TPU v7x, 32 devices: a whole 2x2x4 slice. The times are simulated.
32 devices in a mesh: row: 2 (over x), col: 16 (over z, y, core).
Axes of the slice: x: 2, y: 2, z: 4, core: 2. Of those that a mesh axis runs over, the one named last changes fastest.
Arguments:
- tile_values: float32 [2, 16, 64, 128, 128], P('row', 'col'), may hold values from -0.21875 to 0.21875
- tile_rows: int32 [2, 16, 64], P('row', 'col'), may hold values from 0 to 159, as said below
- tile_cols: int32 [2, 16, 64], P('row', 'col'), may hold values from 0 to 23
- x_start: float32 [384, 128], P('col', 'row'), may hold values from -6 to 6
- z_start: float32 [320, 128], P('row'), may hold values from -6 to 6
- y_start: float32 [320, 128], P('row'), may hold values from -3 to 3
- lower_bound: float32 [320, 128], P('row'), may hold values from -1.5 to -0.1
- upper_bound: float32 [320, 128], P('row'), may hold values from 0.1 to 1.5
- cost_diag: float32 [384, 128], P('col', 'row'), may hold values from 0.1 to 10
- linear: float32 [384, 128], P('col', 'row'), may hold values from -6 to 6
- penalty: float32 [1], replicated, may hold values from 0.3 to 3
- proximal: float32 [1], replicated, may hold values from 0.1 to 1
- relaxation: float32 [1], replicated, may hold values from 1.2 to 1.8
Outputs:
- x_next: float32 [384, 128], P('col', 'row')
- z_next: float32 [320, 128], P('row')
- y_next: float32 [320, 128], P('row')
Inputs may be any that keep to these rules, and one draw needn't show every extreme that they name: On each device the 64 pairs (tile_rows, tile_cols) are distinct.
All inputs are finite; a program needn't handle non-finite values.
Results may differ from a plain program's by a relative error of at most 0.0002.
Values sent between devices are 32-bit elements; how exact they have to be, the bound alone decides.
No kernel may reach another device: no remote copies, remote signals or barrier semaphores. Data moves between devices by JAX's collectives and lax.ppermute only.
A program may use at most 64 MiB of HBM per device.

v0:
```python
import jax
import jax.numpy as jnp
from jax import lax
from jax.sharding import PartitionSpec as P

ADMM_ITERS = 2
HIGH = lax.Precision.HIGHEST


def shards(
    tile_values,
    tile_rows,
    tile_cols,
    x_start,
    z_start,
    y_start,
    lower_bound,
    upper_bound,
    cost_diag,
    linear,
    penalty,
    proximal,
    relaxation,
):
    order_size = tile_values.shape[3]
    flat_tiles = tile_values.reshape(-1, order_size, order_size)
    row_index = tile_rows.reshape(-1)
    col_index = tile_cols.reshape(-1)
    count_tiles = row_index.shape[0]
    block_rows = z_start.shape[0]
    block_cols = x_start.shape[0]
    row_table = (
        lax.broadcasted_iota(jnp.int32, (block_rows, count_tiles), 0) == row_index[None, :]
    ).astype(jnp.float32)
    col_table = (
        lax.broadcasted_iota(jnp.int32, (block_cols, count_tiles), 0) == col_index[None, :]
    ).astype(jnp.float32)
    rho_value = penalty[0]
    sigma_value = proximal[0]
    relax_value = relaxation[0]
    empty_rows = jnp.zeros((block_rows, order_size), jnp.float32)

    def forward_terms(segment):
        picked = jnp.take(segment, col_index, axis=0)
        products = jnp.einsum("kij,kj->ki", flat_tiles, picked, precision=HIGH)
        return jnp.dot(row_table, products, precision=HIGH)

    def apply_forward(vector):
        local_part = forward_terms(lax.all_gather(vector, "row", axis=1, tiled=True))
        return lax.psum(local_part, "col")

    def apply_backward(weights_rows):
        picked = jnp.take(weights_rows, row_index, axis=0)
        products = jnp.einsum("kij,ki->kj", flat_tiles, picked, precision=HIGH)
        local_part = jnp.dot(col_table, products, precision=HIGH)
        return lax.psum_scatter(local_part, "row", scatter_dimension=1, tiled=True)

    def global_totals(values):
        stacked = jnp.stack([jnp.sum(value) for value in values])
        return lax.psum(stacked, ("row", "col"))

    x_now, diag_now, linear_now = (x_start, cost_diag, linear)
    z_now, y_now = (z_start, y_start)
    image_now = empty_rows
    for outer_round in range(ADMM_ITERS):
        if outer_round == 0:
            image_now = apply_forward(x_now)
        target = rho_value * z_now - y_now - rho_value * image_now
        residual = -linear_now - diag_now * x_now + apply_backward(target)
        guess = x_now
        direction = residual
        image_sum = image_now
        norm_now = jnp.float32(1.0)
        norm_now = global_totals([residual * residual])[0]
        pushed = apply_forward(direction)
        applied = (diag_now + sigma_value) * direction + rho_value * apply_backward(pushed)
        curvature = global_totals([direction * applied])[0]
        step_length = norm_now / curvature
        guess = guess + step_length * direction
        image_sum = image_sum + step_length * pushed
        residual = residual - step_length * applied
        image_now = relax_value * image_sum + (1.0 - relax_value) * image_now
        x_now = relax_value * guess + (1.0 - relax_value) * x_now
        mixed = relax_value * image_sum + (1.0 - relax_value) * z_now
        z_fresh = jnp.minimum(jnp.maximum(mixed + y_now / rho_value, lower_bound), upper_bound)
        y_now = y_now + rho_value * (mixed - z_fresh)
        z_now = z_fresh
    return (x_now, z_now, y_now)


def solution(mesh):
    placed = (
        P("row", "col", None, None, None),
        P("row", "col", None),
        P("row", "col", None),
        P("col", "row"),
        P("row", None),
        P("row", None),
        P("row", None),
        P("row", None),
        P("col", "row"),
        P("col", "row"),
        P(),
        P(),
        P(),
    )
    return jax.shard_map(
        shards,
        mesh=mesh,
        in_specs=placed,
        out_specs=(P("col", "row"), P("row", None), P("row", None)),
        check_vma=False,
    )
```

profile of v0, /device:TPU:0, one launch (start us, length us, event | category | flops | bytes accessed | tf_op | source)
XLA Modules:
  0.0 485.3 jit_solution(160176400009086084)
XLA Ops:
  7.2 0.0 all-reduce.6.cloned.1.call-start
  7.2 0.7 compare_select_fusion.1
  7.9 0.7 compare_and_fusion.1
  8.6 5.6 %all-gather = f32[2,64,24]{1,2,0:T(8,128)S(1)} all-gather(f32[1,64,24]{1,2,0:T(8,128)} %bitcast.128), channel_id=1, replica_groups=mesh['row'=2,'col'=16] {'row'}, dimensions={0}, use_global_device_ids=true | all-gather | bytes 18432 | tf_op jit(solution)/shard_map/all_gather | solution.py:49
  14.2 0.1 reshape.90
  14.3 0.6 gather_fusion
  14.9 0.1 broadcast_select_fusion.6
  15.0 8.3 %fusion.12 = f32[64,1,128]{2,1,0:T(1,128)S(1)} fusion(f32[64,128,1]{1,2,0:T(1,128)S(1)} %bitcast.138, f32[1,1,64,128,128]{4,3,2,1,0:T(8,128)} %param.17), kind=kOutput, calls=%fused_computation.19 | convolution fusion | flops 12582912 | bytes 4259840 | tf_op jit(solution)/shard_map/kij,kj->ki/dot_general | solution.py:45
  23.3 0.8 fusion.16
  24.2 0.0 all-reduce.6.cloned.1.call-update
  24.2 0.0 reduce-scatter.13.cloned.1.call-start
  24.9 87.9 %all-reduce.6.cloned.1.call-done = f32[160,128]{1,0:T(8,128)} async-done(((f32[160,128]{1,0:T(8,128)}), f32[160,128]{1,0:T(8,128)}) %all-reduce.6.cloned.1.call-update) | async-done | bytes 81936 | tf_op jit(solution)/shard_map/psum | solution.py:50
  112.9 0.9 multiply_subtract_fusion.1
  113.8 0.6 gather_fusion.1
  114.4 0.1 broadcast_select_fusion.5
  114.4 5.3 %fusion.10 = f32[64,1,128]{2,1,0:T(1,128)S(1)} fusion(f32[64,128,1]{1,2,0:T(1,128)S(1)} %bitcast.139, f32[1,1,64,128,128]{4,3,2,1,0:T(8,128)} %param.17), kind=kOutput, calls=%fused_computation.17 | convolution fusion | flops 12582912 | bytes 4259840 | tf_op jit(solution)/shard_map/kij,ki->kj/dot_general | solution.py:54
  119.7 0.9 convolution_bitcast_fusion.3
  120.6 0.0 reduce-scatter.13.cloned.1.call-update
  120.6 0.0 all-reduce.8.cloned.1.call-start
  120.7 11.1 %reduce-scatter.13.cloned.1.call-done = f32[64,24]{1,0:T(8,128)} async-done(((f32[128,24]{1,0:T(8,128)}), f32[64,24]{1,0:T(8,128)}) %reduce-scatter.13.cloned.1.call-update) | async-done | bytes 6160
  131.8 0.8 copy.38
  132.6 4.4 all-gather.1
  137.0 0.1 reshape.92
  137.1 0.6 gather_fusion.2
  137.7 0.1 broadcast_select_fusion.4
  137.8 8.4 %fusion.8 = f32[64,1,128]{2,1,0:T(1,128)S(1)} fusion(f32[64,128,1]{1,2,0:T(1,128)S(1)} %bitcast.140, f32[1,1,64,128,128]{4,3,2,1,0:T(8,128)} %param.17), kind=kOutput, calls=%fused_computation.15 | convolution fusion | flops 12582912 | bytes 4259840 | tf_op jit(solution)/shard_map/kij,kj->ki/dot_general | solution.py:45
  146.2 0.8 fusion.15
  147.0 0.0 reduce-scatter.15.cloned.1.call-start
  147.1 87.0 %all-reduce.8.cloned.1.call-done = f32[160,128]{1,0:T(8,128)} async-done(((f32[160,128]{1,0:T(8,128)}), f32[160,128]{1,0:T(8,128)}) %all-reduce.8.cloned.1.call-update) | async-done | bytes 81936 | tf_op jit(solution)/shard_map/psum | solution.py:50
  234.0 1.6 gather_fusion.3
  235.6 0.1 broadcast_select_fusion.3
  235.7 5.3 %fusion.6 = f32[64,1,128]{2,1,0:T(1,128)S(1)} fusion(f32[64,128,1]{1,2,0:T(1,128)S(1)} %bitcast.141, f32[1,1,64,128,128]{4,3,2,1,0:T(8,128)} %param.17), kind=kOutput, calls=%fused_computation.13 | convolution fusion | flops 12582912 | bytes 4259840 | tf_op jit(solution)/shard_map/kij,ki->kj/dot_general | solution.py:54
  240.9 0.9 convolution_bitcast_fusion.2
  241.9 0.0 reduce-scatter.17.cloned.1.call-start
  243.2 9.8 %reduce-scatter.15.cloned.1.call-done = f32[64,24]{1,0:T(8,128)} async-done(((f32[128,24]{1,0:T(8,128)}), f32[64,24]{1,0:T(8,128)}) %reduce-scatter.15.cloned.1.call-update) | async-done | bytes 6160
  253.0 0.8 copy.40
  253.8 0.6 multiply_reduce_fusion.2
  254.4 39.7 %all-reduce.1 = (f32[1]{0:T(128)}, f32[1]{0:T(128)}) all-reduce(f32[1]{0:T(128)} %bitcast.16, f32[1]{0:T(128)} %bitcast.29), channel_id=1, replica_groups=mesh['row'=2,'col'=16] {'row','col'}, use_global_device_ids=true, to_apply=%region_3.6 | all-reduce | flops 2 | bytes 16 | tf_op jit(solution)/shard_map/psum | solution.py:60
  295.5 0.1 multiply_subtract_fusion
  295.6 0.6 gather_fusion.4
  296.2 0.1 broadcast_select_fusion.2
  296.3 5.3 %fusion.4 = f32[64,1,128]{2,1,0:T(1,128)S(1)} fusion(f32[64,128,1]{1,2,0:T(1,128)S(1)} %bitcast.142, f32[1,1,64,128,128]{4,3,2,1,0:T(8,128)} %param.17), kind=kOutput, calls=%fused_computation.11 | convolution fusion | flops 12582912 | bytes 4259840 | tf_op jit(solution)/shard_map/kij,ki->kj/dot_general | solution.py:54
  301.5 0.9 convolution_bitcast_fusion.1
  302.5 0.0 all-reduce.10.cloned.1.call-start
  302.5 11.1 %reduce-scatter.17.cloned.1.call-done = f32[64,24]{1,0:T(8,128)} async-done(((f32[128,24]{1,0:T(8,128)}), f32[64,24]{1,0:T(8,128)}) %reduce-scatter.17.cloned.1.call-update) | async-done | bytes 6160
  313.6 0.8 copy.42
  314.4 4.4 all-gather.2
  318.8 0.1 reshape.94
  318.9 0.6 gather_fusion.5
  319.5 0.1 broadcast_select_fusion.1
  319.6 8.3 %fusion.2 = f32[64,1,128]{2,1,0:T(1,128)S(1)} fusion(f32[64,128,1]{1,2,0:T(1,128)S(1)} %bitcast.136, f32[1,1,64,128,128]{4,3,2,1,0:T(8,128)} %param.17), kind=kOutput, calls=%fused_computation.9 | convolution fusion | flops 12582912 | bytes 4259840 | tf_op jit(solution)/shard_map/kij,kj->ki/dot_general | solution.py:45
  327.9 0.8 fusion.14
  328.8 0.0 reduce-scatter.19.cloned.1.call-start
  328.8 87.0 %all-reduce.10.cloned.1.call-done = f32[160,128]{1,0:T(8,128)} async-done(((f32[160,128]{1,0:T(8,128)}), f32[160,128]{1,0:T(8,128)}) %all-reduce.10.cloned.1.call-update) | async-done | bytes 81936 | tf_op jit(solution)/shard_map/psum | solution.py:50
  415.8 1.6 gather_fusion.6
  417.4 0.1 broadcast_select_fusion
  417.4 5.3 %fusion = f32[64,1,128]{2,1,0:T(1,128)S(1)} fusion(f32[64,128,1]{1,2,0:T(1,128)S(1)} %bitcast.137, f32[1,1,64,128,128]{4,3,2,1,0:T(8,128)} %param.17), kind=kOutput, calls=%fused_computation.7 | convolution fusion | flops 12582912 | bytes 4259840 | tf_op jit(solution)/shard_map/kij,ki->kj/dot_general | solution.py:54
  422.7 0.9 convolution_bitcast_fusion
  423.6 11.1 %reduce-scatter.19.cloned.1.call-done = f32[64,24]{1,0:T(8,128)} async-done(((f32[128,24]{1,0:T(8,128)}), f32[64,24]{1,0:T(8,128)}) %reduce-scatter.19.cloned.1.call-update) | async-done | bytes 6160
  434.8 0.8 copy.44
  435.6 0.6 multiply_reduce_fusion
  436.2 39.5 %all-reduce = (f32[1]{0:T(128)}, f32[1]{0:T(128)}) all-reduce(f32[1]{0:T(128)} %bitcast.35, f32[1]{0:T(128)} %bitcast.47), channel_id=1, replica_groups=mesh['row'=2,'col'=16] {'row','col'}, use_global_device_ids=true, to_apply=%region_10.13 | all-reduce | flops 2 | bytes 16 | tf_op jit(solution)/shard_map/psum | solution.py:60
  477.1 0.6 multiply_add_fusion.5
  477.7 0.7 multiply_add_fusion
  (38 shorter events, 0.2 us)
Async XLA Ops:
  7.2 16.2 %copy-start.11 = (s32[1,1,64]{2,1,0:T(1,128)S(1)}, s32[1,1,64]{2,1,0:T(1,128)}, u32[]{:S(2)}) copy-start(s32[1,1,64]{2,1,0:T(1,128)} %param.18) | copy-start | bytes 772
  7.2 105.7 %copy-start.3 = (f32[160,128]{1,0:T(8,128)S(1)}, f32[160,128]{1,0:T(8,128)}, u32[]{:S(2)}) copy-start(f32[160,128]{1,0:T(8,128)} %param.22) | copy-start | bytes 245764
  7.2 105.7 %copy-start.4 = (f32[160,128]{1,0:T(8,128)S(1)}, f32[160,128]{1,0:T(8,128)}, u32[]{:S(2)}) copy-start(f32[160,128]{1,0:T(8,128)} %param.21) | copy-start | bytes 245764
  7.2 105.7 %all-reduce.6.cloned.1.call-start = ((), (), s32[]{:S(2)}) async-start(), calls=%async_computation.4 | async-start | bytes 163840 | tf_op jit(solution)/shard_map/psum | solution.py:50
  15.0 104.8 %copy-start.10 = (s32[1,1,64]{2,1,0:T(1,128)S(1)}, s32[1,1,64]{2,1,0:T(1,128)}, u32[]{:S(2)}) copy-start(s32[1,1,64]{2,1,0:T(1,128)} %param.19) | copy-start | bytes 772
  15.0 117.6 %copy-start.7 = (f32[24,64]{1,0:T(8,128)S(1)}, f32[24,64]{1,0:T(8,128)}, u32[]{:S(2)}) copy-start(f32[24,64]{1,0:T(8,128)} %param.25) | copy-start | bytes 18436
  15.0 117.6 %copy-start.8 = (f32[24,64]{1,0:T(8,128)S(1)}, f32[24,64]{1,0:T(8,128)}, u32[]{:S(2)}) copy-start(f32[24,64]{1,0:T(8,128)} %param.20) | copy-start | bytes 18436
  15.0 117.6 %copy-start.9 = (f32[24,64]{1,0:T(8,128)S(1)}, f32[24,64]{1,0:T(8,128)}, u32[]{:S(2)}) copy-start(f32[24,64]{1,0:T(8,128)} %param.26) | copy-start | bytes 18436
  24.2 107.6 %reduce-scatter.13.cloned.1.call-start = ((), (), s32[]{:S(2)}) async-start(), calls=%async_computation.7 | async-start | bytes 98304
  120.6 113.4 %all-reduce.8.cloned.1.call-start = ((), (), s32[]{:S(2)}) async-start(), calls=%async_computation.5 | async-start | bytes 163840 | tf_op jit(solution)/shard_map/psum | solution.py:50
  137.8 157.7 %copy-start.2 = (f32[160,128]{1,0:T(8,128)S(1)}, f32[160,128]{1,0:T(8,128)}, u32[]{:S(2)}) copy-start(f32[160,128]{1,0:T(8,128)} %all-reduce.6.cloned.1.call-done) | copy-start | bytes 245764
  137.8 157.7 %copy-start.5 = (f32[160,128]{1,0:T(8,128)S(1)}, f32[160,128]{1,0:T(8,128)}, u32[]{:S(2)}) copy-start(f32[160,128]{1,0:T(8,128)} %param.24) | copy-start | bytes 245764
  137.8 157.7 %copy-start.6 = (f32[160,128]{1,0:T(8,128)S(1)}, f32[160,128]{1,0:T(8,128)}, u32[]{:S(2)}) copy-start(f32[160,128]{1,0:T(8,128)} %param.23) | copy-start | bytes 245764
  147.0 106.0 %reduce-scatter.15.cloned.1.call-start = ((), (), s32[]{:S(2)}) async-start(), calls=%async_computation.8 | async-start | bytes 98304
  234.0 61.5 %copy-start = (f32[160,128]{1,0:T(8,128)S(1)}, f32[160,128]{1,0:T(8,128)}, u32[]{:S(2)}) copy-start(f32[160,128]{1,0:T(8,128)} %all-reduce.8.cloned.1.call-done) | copy-start | bytes 245764
  241.9 71.7 %reduce-scatter.17.cloned.1.call-start = ((), (), s32[]{:S(2)}) async-start(), calls=%async_computation.9 | async-start | bytes 98304
  302.5 113.4 %all-reduce.10.cloned.1.call-start = ((), (), s32[]{:S(2)}) async-start(), calls=%async_computation.6 | async-start | bytes 163840 | tf_op jit(solution)/shard_map/psum | solution.py:50
  328.8 106.0 %reduce-scatter.19.cloned.1.call-start = ((), (), s32[]{:S(2)}) async-start(), calls=%async_computation.10 | async-start | bytes 98304
  415.8 61.9 %copy-start.1 = (f32[160,128]{1,0:T(8,128)S(1)}, f32[160,128]{1,0:T(8,128)}, u32[]{:S(2)}) copy-start(f32[160,128]{1,0:T(8,128)} %all-reduce.10.cloned.1.call-done) | copy-start | bytes 245764
Sparse Core Ops, SparseCore 0:
  24.3 88.5 all-reduce.5
  120.8 10.9 reduce-scatter.12
  147.1 86.8 all-reduce.7
  242.0 10.9 reduce-scatter.14
  302.6 10.9 reduce-scatter.16
  328.9 86.8 all-reduce.9
  423.8 10.9 reduce-scatter.18
where the time goes:
time: 486 us; the launch traced here: 485 us
  waiting for transfers between devices  305 us (63%)
  blocking collectives  93.6 us (19%)
  matrix products  52.1 us (11%)
  between operations  19 us (4%)
  local copies, waits for them, and re-layouts  9.73 us (2%)
  other arithmetic  5.46 us (1%)
    psum x3, waiting for transfers between devices, apply_forward(): return lax.psum(local_part, 'col')  262 us
    psum x2, blocking collectives, global_totals(): return lax.psum(stacked, ('row', 'col'))  79.3 us
    unnamed x11, waiting for transfers between devices  43.1 us
    dot_general x3, matrix products, forward_terms(): products = jnp.einsum('kij,kj->ki', flat_tiles, picked, precision=HIGH)  25 us
    dot_general x4, matrix products, apply_backward(): products = jnp.einsum('kij,ki->kj', flat_tiles, picked, precision=HIGH)  21.1 us
    all_gather x3, blocking collectives, apply_forward(): lax.all_gather(vector, 'row', axis=1, tiled=True)  14.4 us
  transfers between devices with their start and end apart: 7, of which 7 were waited for; matrix products, arithmetic and copies ran while one was open for 0% of the time, Pallas kernels for 0%

commit v1 on v0

--- a/solution.py
+++ b/solution.py
@@ -5,6 +5,11 @@
 
 ADMM_ITERS = 2
 HIGH = lax.Precision.HIGHEST
+
+
+def _draw_slices(body, axis_id):
+    part_next = jnp.sum(lax.all_gather(body, axis_name=axis_id), axis=0)
+    return part_next
 
 
 def shards(
@@ -57,7 +62,7 @@
 
     def global_totals(values):
         stacked = jnp.stack([jnp.sum(value) for value in values])
-        return lax.psum(stacked, ("row", "col"))
+        return _draw_slices(stacked, axis_id=("row", "col"))
 
     x_now, diag_now, linear_now = (x_start, cost_diag, linear)
     z_now, y_now = (z_start, y_start)

time: 486 us -> 491 us (1.010)
    psum x2 -> x0, blocking collectives: 79.3 us -> none  [global_totals(): return lax.psum(stacked, ('row', 'col'))]
    unnamed x0 -> x2, blocking collectives: none -> 78.7 us
where the time goes in v1:
time: 491 us; the launch traced here: 490 us
  waiting for transfers between devices  305 us (62%)
  blocking collectives  93.1 us (19%)
  matrix products  52.1 us (11%)
  between operations  19 us (4%)
  local copies, waits for them, and re-layouts  12.8 us (3%)
  other arithmetic  7.85 us (2%)
    psum x3, waiting for transfers between devices, apply_forward(): return lax.psum(local_part, 'col')  262 us
    unnamed x2, blocking collectives  78.7 us
    unnamed x11, waiting for transfers between devices  42.9 us
    dot_general x3, matrix products, forward_terms(): products = jnp.einsum('kij,kj->ki', flat_tiles, picked, precision=HIGH)  25 us
    dot_general x4, matrix products, apply_backward(): products = jnp.einsum('kij,ki->kj', flat_tiles, picked, precision=HIGH)  21.1 us
    all_gather x3, blocking collectives, apply_forward(): lax.all_gather(vector, 'row', axis=1, tiled=True)  14.4 us
  transfers between devices with their start and end apart: 7, of which 7 were waited for; matrix products, arithmetic and copies ran while one was open for 0% of the time, Pallas kernels for 0%

profile of v1, /device:TPU:0, one launch (start us, length us, event | category | flops | bytes accessed | tf_op | source)
XLA Modules:
  0.0 489.8 jit_solution(1402416280201542845)
XLA Ops:
  7.2 0.7 compare_select_fusion.1
  7.9 0.7 compare_and_fusion.1
  8.6 5.6 %all-gather = f32[2,64,24]{1,2,0:T(8,128)S(1)} all-gather(f32[1,64,24]{1,2,0:T(8,128)} %bitcast.126), channel_id=1, replica_groups=mesh['row'=2,'col'=16] {'row'}, dimensions={0}, use_global_device_ids=true | all-gather | bytes 18432 | tf_op jit(solution)/shard_map/all_gather | solution.py:54
  14.2 0.1 reshape.104
  14.3 0.6 gather_fusion
  14.9 0.1 broadcast_select_fusion.6
  15.0 8.3 %fusion.12 = f32[64,1,128]{2,1,0:T(1,128)S(1)} fusion(f32[64,128,1]{1,2,0:T(1,128)S(1)} %bitcast.136, f32[1,1,64,128,128]{4,3,2,1,0:T(8,128)} %param.17), kind=kOutput, calls=%fused_computation.19 | convolution fusion | flops 12582912 | bytes 4259840 | tf_op jit(solution)/shard_map/kij,kj->ki/dot_general | solution.py:50
  23.3 0.8 fusion.16
  24.9 87.9 %all-reduce.10.cloned.1.call-done = f32[160,128]{1,0:T(8,128)} async-done(((f32[160,128]{1,0:T(8,128)}), f32[160,128]{1,0:T(8,128)}) %all-reduce.10.cloned.1.call-update) | async-done | bytes 81936 | tf_op jit(solution)/shard_map/psum | solution.py:55
  112.8 0.9 multiply_subtract_fusion.1
  113.7 0.6 gather_fusion.1
  114.3 0.1 broadcast_select_fusion.5
  114.4 5.3 %fusion.10 = f32[64,1,128]{2,1,0:T(1,128)S(1)} fusion(f32[64,128,1]{1,2,0:T(1,128)S(1)} %bitcast.137, f32[1,1,64,128,128]{4,3,2,1,0:T(8,128)} %param.17), kind=kOutput, calls=%fused_computation.17 | convolution fusion | flops 12582912 | bytes 4259840 | tf_op jit(solution)/shard_map/kij,ki->kj/dot_general | solution.py:59
  119.6 0.9 convolution_bitcast_fusion.3
  120.6 11.1 %reduce-scatter.13.cloned.1.call-done = f32[64,24]{1,0:T(8,128)} async-done(((f32[128,24]{1,0:T(8,128)}), f32[64,24]{1,0:T(8,128)}) %reduce-scatter.13.cloned.1.call-update) | async-done | bytes 6160
  131.7 0.8 copy.38
  132.5 4.4 all-gather.1
  136.9 0.1 reshape.106
  137.0 0.6 gather_fusion.2
  137.6 0.1 broadcast_select_fusion.4
  137.7 8.4 %fusion.8 = f32[64,1,128]{2,1,0:T(1,128)S(1)} fusion(f32[64,128,1]{1,2,0:T(1,128)S(1)} %bitcast.138, f32[1,1,64,128,128]{4,3,2,1,0:T(8,128)} %param.17), kind=kOutput, calls=%fused_computation.15 | convolution fusion | flops 12582912 | bytes 4259840 | tf_op jit(solution)/shard_map/kij,kj->ki/dot_general | solution.py:50
  146.1 0.8 fusion.15
  146.9 0.0 reduce-scatter.15.cloned.1.call-start
  147.0 87.0 %all-reduce.12.cloned.1.call-done = f32[160,128]{1,0:T(8,128)} async-done(((f32[160,128]{1,0:T(8,128)}), f32[160,128]{1,0:T(8,128)}) %all-reduce.12.cloned.1.call-update) | async-done | bytes 81936 | tf_op jit(solution)/shard_map/psum | solution.py:55
  234.0 1.6 gather_fusion.3
  235.6 0.1 broadcast_select_fusion.3
  235.6 5.3 %fusion.6 = f32[64,1,128]{2,1,0:T(1,128)S(1)} fusion(f32[64,128,1]{1,2,0:T(1,128)S(1)} %bitcast.139, f32[1,1,64,128,128]{4,3,2,1,0:T(8,128)} %param.17), kind=kOutput, calls=%fused_computation.13 | convolution fusion | flops 12582912 | bytes 4259840 | tf_op jit(solution)/shard_map/kij,ki->kj/dot_general | solution.py:59
  240.9 0.9 convolution_bitcast_fusion.2
  243.2 9.8 %reduce-scatter.15.cloned.1.call-done = f32[64,24]{1,0:T(8,128)} async-done(((f32[128,24]{1,0:T(8,128)}), f32[64,24]{1,0:T(8,128)}) %reduce-scatter.15.cloned.1.call-update) | async-done | bytes 6160
  252.9 0.8 copy.40
  253.8 0.6 multiply_reduce_fusion.2
  254.4 0.8 dynamic-update-slice
  255.1 0.8 dynamic-update-slice.1
  255.9 39.4 %all-reduce.5 = (f32[32]{0:T(128)S(1)}, f32[32]{0:T(128)S(1)}) all-reduce(f32[32]{0:T(128)S(1)} %dynamic-update-slice, f32[32]{0:T(128)S(1)} %dynamic-update-slice.1), channel_id=1, replica_groups=mesh['row'=2,'col'=16] {'row','col'}, use_global_device_ids=true, to_apply=%add | all-reduce | flops 64 | bytes 512
  295.3 0.6 reduce.4
  295.9 0.6 reduce.5
  297.9 0.1 multiply_subtract_fusion
  298.0 0.6 gather_fusion.4
  298.6 0.1 broadcast_select_fusion.2
  298.7 5.3 %fusion.4 = f32[64,1,128]{2,1,0:T(1,128)S(1)} fusion(f32[64,128,1]{1,2,0:T(1,128)S(1)} %bitcast.140, f32[1,1,64,128,128]{4,3,2,1,0:T(8,128)} %param.17), kind=kOutput, calls=%fused_computation.11 | convolution fusion | flops 12582912 | bytes 4259840 | tf_op jit(solution)/shard_map/kij,ki->kj/dot_general | solution.py:59
  303.9 0.9 convolution_bitcast_fusion.1
  304.9 10.9 %reduce-scatter.17.cloned.1.call-done = f32[64,24]{1,0:T(8,128)} async-done(((f32[128,24]{1,0:T(8,128)}), f32[64,24]{1,0:T(8,128)}) %reduce-scatter.17.cloned.1.call-update) | async-done | bytes 6160
  315.8 0.8 copy.42
  316.6 4.4 all-gather.2
  321.1 0.1 reshape.108
  321.1 0.6 gather_fusion.5
  321.7 0.1 broadcast_select_fusion.1
  321.8 8.3 %fusion.2 = f32[64,1,128]{2,1,0:T(1,128)S(1)} fusion(f32[64,128,1]{1,2,0:T(1,128)S(1)} %bitcast.134, f32[1,1,64,128,128]{4,3,2,1,0:T(8,128)} %param.17), kind=kOutput, calls=%fused_computation.9 | convolution fusion | flops 12582912 | bytes 4259840 | tf_op jit(solution)/shard_map/kij,kj->ki/dot_general | solution.py:50
  330.1 0.8 fusion.14
  331.0 86.9 %all-reduce.14.cloned.1.call-done = f32[160,128]{1,0:T(8,128)} async-done(((f32[160,128]{1,0:T(8,128)}), f32[160,128]{1,0:T(8,128)}) %all-reduce.14.cloned.1.call-update) | async-done | bytes 81936 | tf_op jit(solution)/shard_map/psum | solution.py:55
  418.0 1.6 gather_fusion.6
  419.5 0.1 broadcast_select_fusion
  419.6 5.3 %fusion = f32[64,1,128]{2,1,0:T(1,128)S(1)} fusion(f32[64,128,1]{1,2,0:T(1,128)S(1)} %bitcast.135, f32[1,1,64,128,128]{4,3,2,1,0:T(8,128)} %param.17), kind=kOutput, calls=%fused_computation.7 | convolution fusion | flops 12582912 | bytes 4259840 | tf_op jit(solution)/shard_map/kij,ki->kj/dot_general | solution.py:59
  424.9 0.9 convolution_bitcast_fusion
  425.8 11.1 %reduce-scatter.19.cloned.1.call-done = f32[64,24]{1,0:T(8,128)} async-done(((f32[128,24]{1,0:T(8,128)}), f32[64,24]{1,0:T(8,128)}) %reduce-scatter.19.cloned.1.call-update) | async-done | bytes 6160
  436.9 0.8 copy.44
  437.7 0.6 multiply_reduce_fusion
  438.3 0.8 dynamic-update-slice.2
  439.1 0.8 dynamic-update-slice.3
  439.8 39.3 %all-reduce.4 = (f32[32]{0:T(128)S(1)}, f32[32]{0:T(128)S(1)}) all-reduce(f32[32]{0:T(128)S(1)} %dynamic-update-slice.2, f32[32]{0:T(128)S(1)} %dynamic-update-slice.3), channel_id=1, replica_groups=mesh['row'=2,'col'=16] {'row','col'}, use_global_device_ids=true, to_apply=%add.2 | all-reduce | flops 64 | bytes 512
  479.1 0.6 reduce.6
  479.7 0.6 reduce.7
  481.6 0.6 multiply_add_fusion.5
  482.3 0.7 multiply_add_fusion
  (50 shorter events, 0.5 us)
Async XLA Ops:
  7.2 16.2 %copy-start.11 = (s32[1,1,64]{2,1,0:T(1,128)S(1)}, s32[1,1,64]{2,1,0:T(1,128)}, u32[]{:S(2)}) copy-start(s32[1,1,64]{2,1,0:T(1,128)} %param.18) | copy-start | bytes 772
  7.2 105.6 %copy-start.3 = (f32[160,128]{1,0:T(8,128)S(1)}, f32[160,128]{1,0:T(8,128)}, u32[]{:S(2)}) copy-start(f32[160,128]{1,0:T(8,128)} %param.22) | copy-start | bytes 245764
  7.2 105.6 %copy-start.4 = (f32[160,128]{1,0:T(8,128)S(1)}, f32[160,128]{1,0:T(8,128)}, u32[]{:S(2)}) copy-start(f32[160,128]{1,0:T(8,128)} %param.21) | copy-start | bytes 245764
  7.2 105.6 %all-reduce.10.cloned.1.call-start = ((), (), s32[]{:S(2)}) async-start(), calls=%async_computation.4 | async-start | bytes 163840 | tf_op jit(solution)/shard_map/psum | solution.py:55
  15.0 104.7 %copy-start.10 = (s32[1,1,64]{2,1,0:T(1,128)S(1)}, s32[1,1,64]{2,1,0:T(1,128)}, u32[]{:S(2)}) copy-start(s32[1,1,64]{2,1,0:T(1,128)} %param.19) | copy-start | bytes 772
  15.0 117.5 %copy-start.7 = (f32[24,64]{1,0:T(8,128)S(1)}, f32[24,64]{1,0:T(8,128)}, u32[]{:S(2)}) copy-start(f32[24,64]{1,0:T(8,128)} %param.25) | copy-start | bytes 18436
  15.0 117.5 %copy-start.8 = (f32[24,64]{1,0:T(8,128)S(1)}, f32[24,64]{1,0:T(8,128)}, u32[]{:S(2)}) copy-start(f32[24,64]{1,0:T(8,128)} %param.20) | copy-start | bytes 18436
  15.0 117.5 %copy-start.9 = (f32[24,64]{1,0:T(8,128)S(1)}, f32[24,64]{1,0:T(8,128)}, u32[]{:S(2)}) copy-start(f32[24,64]{1,0:T(8,128)} %param.26) | copy-start | bytes 18436
  24.2 107.5 %reduce-scatter.13.cloned.1.call-start = ((), (), s32[]{:S(2)}) async-start(), calls=%async_computation.7 | async-start | bytes 98304
  120.6 113.5 %all-reduce.12.cloned.1.call-start = ((), (), s32[]{:S(2)}) async-start(), calls=%async_computation.5 | async-start | bytes 163840 | tf_op jit(solution)/shard_map/psum | solution.py:55
  137.7 160.2 %copy-start.2 = (f32[160,128]{1,0:T(8,128)S(1)}, f32[160,128]{1,0:T(8,128)}, u32[]{:S(2)}) copy-start(f32[160,128]{1,0:T(8,128)} %all-reduce.10.cloned.1.call-done) | copy-start | bytes 245764
  137.7 160.2 %copy-start.5 = (f32[160,128]{1,0:T(8,128)S(1)}, f32[160,128]{1,0:T(8,128)}, u32[]{:S(2)}) copy-start(f32[160,128]{1,0:T(8,128)} %param.24) | copy-start | bytes 245764
  137.7 160.2 %copy-start.6 = (f32[160,128]{1,0:T(8,128)S(1)}, f32[160,128]{1,0:T(8,128)}, u32[]{:S(2)}) copy-start(f32[160,128]{1,0:T(8,128)} %param.23) | copy-start | bytes 245764
  146.9 106.0 %reduce-scatter.15.cloned.1.call-start = ((), (), s32[]{:S(2)}) async-start(), calls=%async_computation.8 | async-start | bytes 98304
  234.0 63.9 %copy-start = (f32[160,128]{1,0:T(8,128)S(1)}, f32[160,128]{1,0:T(8,128)}, u32[]{:S(2)}) copy-start(f32[160,128]{1,0:T(8,128)} %all-reduce.12.cloned.1.call-done) | copy-start | bytes 245764
  241.8 74.0 %reduce-scatter.17.cloned.1.call-start = ((), (), s32[]{:S(2)}) async-start(), calls=%async_computation.9 | async-start | bytes 98304
  304.9 113.1 %all-reduce.14.cloned.1.call-start = ((), (), s32[]{:S(2)}) async-start(), calls=%async_computation.6 | async-start | bytes 163840 | tf_op jit(solution)/shard_map/psum | solution.py:55
  331.0 105.9 %reduce-scatter.19.cloned.1.call-start = ((), (), s32[]{:S(2)}) async-start(), calls=%async_computation.10 | async-start | bytes 98304
  417.9 64.3 %copy-start.1 = (f32[160,128]{1,0:T(8,128)S(1)}, f32[160,128]{1,0:T(8,128)}, u32[]{:S(2)}) copy-start(f32[160,128]{1,0:T(8,128)} %all-reduce.14.cloned.1.call-done) | copy-start | bytes 245764
Sparse Core Ops, SparseCore 0:
  24.3 88.4 all-reduce.9
  120.7 10.9 reduce-scatter.12
  147.1 86.9 all-reduce.11
  242.0 10.9 reduce-scatter.14
  305.0 10.7 reduce-scatter.16
  331.1 86.8 all-reduce.13
  425.9 10.9 reduce-scatter.18
